TPU v7x, 32 devices: a whole 2x2x4 slice. The times are simulated.
32 devices in a mesh: groups: 2 (over x), rows: 16 (over z, y, core).
Axes of the slice: x: 2, y: 2, z: 4, core: 2. Of those that a mesh axis runs over, the one named last changes fastest.
Arguments:
- block_input: bfloat16 [512, 352, 512], P(('groups', 'rows')), parts along dimension 0, may hold values from -6 to 6
- first_pre: bfloat16 [512, 352, 128], P(('groups', 'rows')), parts along dimension 0, may hold values from -6 to 6
- second_pre: bfloat16 [512, 352, 128], P(('groups', 'rows')), parts along dimension 0, may hold values from -6 to 6
- output_pre: bfloat16 [512, 352, 512], P(('groups', 'rows')), parts along dimension 0, may hold values from -6 to 6
- output_grad: bfloat16 [512, 352, 512], P('groups', None, 'rows'), parts along dimension 0, may hold values from -6 to 6
- first_weight: bfloat16 [512, 128], replicated, may hold values from -0.25 to 0.25
- middle_weight: bfloat16 [3, 3, 128, 128], replicated, may hold values from -0.1875 to 0.1875
- last_weight: bfloat16 [128, 512], replicated, may hold values from -0.5 to 0.5
Outputs:
- input_grad: bfloat16 [512, 352, 512], P(('groups', 'rows')), parts along dimension 0
- first_weight_grad: float32 [1024, 128], P(('groups', 'rows')), parts along dimension 0
- middle_weight_grad: float32 [6, 3, 128, 128], P('groups'), parts along dimension 0
- last_weight_grad: float32 [256, 512], P('groups'), parts along dimension 0
There are 2 independent parts, one for each index of `groups`. A program takes and returns all parts, laid end to end along the dimension named above; an argument that names none is the same for every part. Nothing has to cross between parts.
All inputs are finite; a program needn't handle non-finite values.
Results may differ from a plain program's by a relative error of at most 0.0049.
Values may be sent and summed in bfloat16 or wider, within the bound.
No kernel may reach another device: no remote copies, remote signals or barrier semaphores. Data moves between devices by JAX's collectives and lax.ppermute only.
A program may use at most 128 MiB of HBM per device.

v0:
```python
import math
import jax
import jax.numpy as jnp
from jax import lax
from jax.sharding import PartitionSpec as P


def with_halo(value, sides, width):
    for axis, dim in sides:
        size, length = (lax.axis_size(axis), value.shape[dim])
        up = [(i, (i + 1) % size) for i in range(size - 1)]
        down = [(j, i) for i, j in up]
        last = lax.slice_in_dim(value, length - width, length, axis=dim)
        leading = lax.slice_in_dim(value, 0, width, axis=dim)
        before = lax.ppermute(last, axis, up)
        after = lax.ppermute(leading, axis, down)
        value = jnp.concatenate([before, value, after], axis=dim)
    return value


def contract_rows(left, right):
    return lax.dot_general(
        left, right, (((0,), (0,)), ((), ())), preferred_element_type=jnp.float32
    )


def shards(
    block_input,
    first_pre,
    second_pre,
    output_pre,
    output_grad,
    first_weight,
    middle_weight,
    last_weight,
):
    tile_rows, map_cols, channels = block_input.shape
    inner_width = first_pre.shape[2]
    pixels = tile_rows * map_cols
    factor = 1.0 / math.sqrt(pixels * lax.axis_size("rows"))
    spatial = lax.all_to_all(output_grad, "rows", split_axis=0, concat_axis=2, tiled=True)
    masked_out = jnp.where(output_pre > 0, spatial, jnp.zeros_like(spatial))
    second_act = jnp.maximum(second_pre, jnp.zeros_like(second_pre))
    first_act = jnp.maximum(first_pre, jnp.zeros_like(first_pre))
    out_flat = masked_out.reshape(pixels, channels)
    last_part = contract_rows(second_act.reshape(pixels, inner_width), out_flat)
    last_total = lax.psum(last_part, "rows")
    inner = lax.dot_general(
        out_flat, last_weight, (((1,), (1,)), ((), ())), preferred_element_type=jnp.float32
    )
    second_grad = jnp.where(second_pre.reshape(pixels, inner_width) > 0, inner, 0.0).astype(
        jnp.bfloat16
    )
    second_flat = second_grad
    second_grad = second_flat.reshape(tile_rows, map_cols, inner_width)
    act_ext = with_halo(first_act, (("rows", 0),), 1)
    act_padded = jnp.pad(act_ext, ((0, 0), (1, 1), (0, 0)))
    taps = []
    for row_tap in range(3):
        line = []
        for col_tap in range(3):
            window = act_padded[
                row_tap : row_tap + tile_rows, col_tap : col_tap + map_cols
            ].reshape(pixels, inner_width)
            line.append(contract_rows(window, second_flat))
        taps.append(jnp.stack(line))
    middle_part = jnp.stack(taps)
    grad_ext = with_halo(second_grad, (("rows", 0),), 1)
    grad_padded = jnp.pad(grad_ext, ((0, 0), (1, 1), (0, 0)))
    total = jnp.zeros((pixels, inner_width), jnp.float32)
    for row_tap in range(3):
        for col_tap in range(3):
            moved = grad_padded[
                2 - row_tap : 2 - row_tap + tile_rows, 2 - col_tap : 2 - col_tap + map_cols
            ].reshape(pixels, inner_width)
            total = total + lax.dot_general(
                moved,
                middle_weight[row_tap, col_tap],
                (((1,), (1,)), ((), ())),
                preferred_element_type=jnp.float32,
            )
    first_grad = jnp.where(first_pre.reshape(pixels, inner_width) > 0, total, 0.0).astype(
        jnp.bfloat16
    )
    input_flat = block_input.reshape(pixels, channels)
    first_wgrad = (
        lax.psum_scatter(
            contract_rows(input_flat, first_grad), "rows", scatter_dimension=0, tiled=True
        )
        * factor
    )
    back = lax.dot_general(
        first_grad, first_weight, (((1,), (1,)), ((), ())), preferred_element_type=jnp.float32
    )
    input_grad = (
        (back + out_flat.astype(jnp.float32))
        .astype(jnp.bfloat16)
        .reshape(tile_rows, map_cols, channels)
    )
    middle_total = lax.psum(middle_part, "rows")
    return (input_grad, first_wgrad, middle_total * factor, last_total * factor)


def solution(mesh):
    placed = (
        P(("groups", "rows"), None, None),
        P(("groups", "rows"), None, None),
        P(("groups", "rows"), None, None),
        P(("groups", "rows"), None, None),
        P("groups", None, "rows"),
        P(),
        P(),
        P(),
    )
    return jax.shard_map(
        shards,
        mesh=mesh,
        in_specs=placed,
        out_specs=(
            P(("groups", "rows"), None, None),
            P(("groups", "rows"), None),
            P("groups", None, None, None),
            P("groups", None),
        ),
        check_vma=False,
    )
```

profile of v0, /device:TPU:0, one launch (start us, length us, event | category | flops | bytes accessed | tf_op | source)
XLA Modules:
  0.0 376.6 jit_solution(985985323894171516)
XLA Ops:
  7.2 9.7 %copy.21 = bf16[256,352,32]{1,2,0:T(8,128)(2,1)} copy(bf16[256,352,32]{0,2,1:T(8,128)(2,1)} %param.12) | data formatting | bytes 11534336 | tf_op args[4]
  16.8 7.6 %all-to-all-start = ((bf16[256,352,32]{1,2,0:T(8,128)(2,1)}), bf16[256,352,32]{1,2,0:T(8,128)(2,1)}, u32[]{:S(2)}, u32[]{:S(2)}) async-start(bf16[256,352,32]{1,2,0:T(8,128)(2,1)} %copy.21), calls=%async_computation | async-start | bytes 12582912 | tf_op jit(solution)/shard_map/all_to_all | solution.py:41
  24.6 2.4 collective-permute-start.2
  27.0 1.3 collective-permute-start.3
  28.3 1.3 broadcast_compare_fusion.1
  29.6 1.3 broadcast_compare_fusion
  30.9 8.3 %copy.20 = bf16[16,352,512]{1,2,0:T(8,128)(2,1)} copy(bf16[16,352,512]{2,1,0:T(8,128)(2,1)} %param.11) | data formatting | bytes 11534336 | tf_op args[3]
  39.2 1.7 pad_maximum_fusion.1
  41.4 3.9 %fusion.33 = (bf16[16,352,128]{2,1,0:T(8,128)(2,1)}, bf16[16,352,128]{2,1,0:T(8,128)(2,1)}, bf16[16,352,128]{2,1,0:T(8,128)(2,1)}, bf16[16,352,128]{2,1,0:T(8,12...) fusion(bf16[18,354,128]{2,1,0:T(8,128)(2,1)S(1)} %select_maximum_fusion), kind=kLoop, calls=%fused_computation.73 | loop fusion | bytes 17301504 | tf_op jit(solution)/shard_map/slice | solution.py:62
  45.3 93.3 %all-to-all-done = bf16[256,352,32]{1,2,0:T(8,128)(2,1)} async-done(((bf16[256,352,32]{1,2,0:T(8,128)(2,1)}), bf16[256,352,32]{1,2,0:T(8,128)(2,1)}, u32[]{:S(2)}, u32[]{:S(2)}) %all-to-all-start) | async-done | bytes 5767200 | tf_op jit(solution)/shard_map/all_to_all | solution.py:41
  138.6 6.4 %copy.22 = bf16[16,352,16,32]{1,3,2,0:T(8,128)(2,1)} copy(bf16[16,352,16,32]{1,3,0,2:T(8,128)(2,1)} %bitcast.3) | data formatting | bytes 11534336 | tf_op jit(solution)/shard_map/all_to_all | solution.py:41
  145.0 8.0 %compare_select_fusion = bf16[16,352,512]{1,2,0:T(8,128)(2,1)} fusion(bf16[16,352,512]{1,2,0:T(8,128)(2,1)} %copy.20, bf16[16,352,16,32]{1,3,2,0:T(8,128)(2,1)} %copy.22), kind=kLoop, calls=%fused_computation | loop fusion | flops 5767168 | bytes 17301504 | tf_op jit(solution)/shard_map/jit(_where)/select_n | solution.py:42
  153.1 8.5 %copy.23 = bf16[16,352,512]{2,1,0:T(8,128)(2,1)} copy(bf16[16,352,512]{1,2,0:T(8,128)(2,1)} %compare_select_fusion) | data formatting | bytes 11534336 | tf_op jit(solution)/shard_map/jit(_where)/select_n | solution.py:42
  161.6 5.8 %fusion.8 = f32[128,512]{1,0:T(8,128)} fusion(bf16[16,352,512]{1,2,0:T(8,128)(2,1)} %compare_select_fusion, bf16[16,352,128]{2,1,0:T(8,128)(2,1)S(1)} %copy-done.12), kind=kOutput, calls=%fused_computation.28 | convolution fusion | flops 738918400 | bytes 7471104 | tf_op jit(solution)/shard_map/dot_general | solution.py:22
  167.5 1.7 fusion.3
  169.2 0.6 convolution_bitcast_fusion.4
  169.8 0.7 copy-done.9
  170.5 0.6 convolution_bitcast_fusion.6
  171.1 0.8 copy-done.8
  171.9 0.6 convolution_bitcast_fusion.7
  172.5 0.8 copy-done.7
  173.3 0.6 convolution_bitcast_fusion.9
  173.8 0.8 copy-done.4
  174.6 0.6 convolution_bitcast_fusion.8
  175.2 0.6 convolution_bitcast_fusion.5
  175.8 0.8 copy-done.6
  176.6 0.6 convolution_bitcast_fusion.1
  177.2 0.8 copy-done.5
  177.9 0.6 convolution_bitcast_fusion.3
  178.5 0.8 copy-done.3
  179.3 0.6 convolution_bitcast_fusion.2
  179.9 2.7 collective-permute-start
  182.6 1.3 collective-permute-start.1
  183.9 0.9 pad_maximum_fusion.4
  185.0 8.5 %collective-permute-done.1 = bf16[1,352,128]{2,1,0:T(8,128)(2,1)S(1)} collective-permute-done((bf16[1,352,128]{2,1,0:T(8,128)(2,1)S(1)}, bf16[1,352,128]{2,1,0:T(8,128)(2,1)S(1)}, u32[]{:S(2)}, u32[]{:S(2)}) %collective-permute-start.1) | collective-permute-done | bytes 90144 | tf_op jit(solution)/shard_map/ppermute | solution.py:16
  194.1 2.4 fusion.34
  198.3 0.6 convolution_add_fusion.4
  201.6 0.8 fusion.2
  202.9 0.7 slice-done.1
  203.6 1.0 convolution_bitcast_fusion
  204.6 0.8 copy.27
  205.5 6.8 %add_convert_fusion = bf16[5632,512]{1,0:T(8,128)(2,1)} fusion(bf16[5632,512]{1,0:T(8,128)(2,1)} %bitcast.124, bf16[5632,128]{1,0:T(8,128)(2,1)S(1)} %fusion.2, bf16[512,128]{1,0:T(8,128)(2,1)S(1)} %copy-done), kind=kOutput, calls=%fused_computation.1 | convolution fusion | flops 746848256 | bytes 13107200 | tf_op jit(solution)/shard_map/dot_general | solution.py:92
  212.3 97.3 %all-reduce.5.cloned.1.call-done = (f32[3,3,128,128]{3,2,1,0:T(8,128)}, f32[128,512]{1,0:T(8,128)}) async-done(((f32[3,3,128,128]{3,2,1,0:T(8,128)}, f32[128,512]{1,0:T(8,128)}), (f32[3,3,128,128]{3,2,1,0:T(8,128)}, f32[128,512]{1,0:T(8,128)})) %all-reduce.5.cloned.1.call-update) | async-done | bytes 851984 | tf_op jit(solution)/shard_map/psum | solution.py:100
  309.6 1.7 broadcast_multiply_fusion.1
  311.3 1.9 broadcast_multiply_fusion
  313.2 55.1 %reduce-scatter.4.cloned.1.call-done = f32[32,128]{1,0:T(8,128)} async-done(((f32[512,128]{1,0:T(8,128)}), f32[32,128]{1,0:T(8,128)}) %reduce-scatter.4.cloned.1.call-update) | async-done | bytes 16400
  368.2 0.8 copy.28
  369.1 0.7 copy.25
  (54 shorter events, 6.5 us)
Async XLA Ops:
  7.2 198.3 %copy-start = (bf16[512,128]{1,0:T(8,128)(2,1)S(1)}, bf16[512,128]{1,0:T(8,128)(2,1)}, u32[]{:S(2)}) copy-start(bf16[512,128]{1,0:T(8,128)(2,1)} %param.13) | copy-start | bytes 393220
  16.8 7.6 %copy-start.2 = (bf16[16,352,128]{2,1,0:T(8,128)(2,1)S(1)}, bf16[16,352,128]{2,1,0:T(8,128)(2,1)}, u32[]{:S(2)}) copy-start(bf16[16,352,128]{2,1,0:T(8,128)(2,1)} %param.9) | copy-start | bytes 4325380
  16.8 121.8 %all-to-all-start = ((bf16[256,352,32]{1,2,0:T(8,128)(2,1)}), bf16[256,352,32]{1,2,0:T(8,128)(2,1)}, u32[]{:S(2)}, u32[]{:S(2)}) async-start(bf16[256,352,32]{1,2,0:T(8,128)(2,1)} %copy.21), calls=%async_computation | async-start | bytes 12582912 | tf_op jit(solution)/shard_map/all_to_all | solution.py:41
  24.4 285.2 %all-reduce.5.cloned.1.call-start = ((), (), s32[]{:S(2)}) async-start(), calls=%async_computation.3 | async-start | bytes 1703936 | tf_op jit(solution)/shard_map/psum | solution.py:100
  24.6 5.0 %copy-start.11 = (bf16[16,352,128]{2,1,0:T(8,128)(2,1)S(1)}, bf16[16,352,128]{2,1,0:T(8,128)(2,1)}, u32[]{:S(2)}) copy-start(bf16[16,352,128]{2,1,0:T(8,128)(2,1)} %param.10) | copy-start | bytes 4325380
  24.6 14.6 %collective-permute-start.2 = (bf16[1,352,128]{2,1,0:T(8,128)(2,1)S(1)}, bf16[1,352,128]{2,1,0:T(8,128)(2,1)S(1)}, u32[]{:S(2)}, u32[]{:S(2)}) collective-permute-start(bf16[1,352,128]{2,1,0:T(8,128)(2,1)S(1)} %get-tuple-element.32), channel_id=1, source_target_pairs={{0,1},{1,2},{2,3},{3,4},{4,5},{5,6},{6,7},{7,8},{8,9},{9,10},{10,1... | collective-permute-start | bytes 270344 | tf_op jit(solution)/shard_map/ppermute | solution.py:15
  27.0 12.2 %collective-permute-start.3 = (bf16[1,352,128]{2,1,0:T(8,128)(2,1)S(1)}, bf16[1,352,128]{2,1,0:T(8,128)(2,1)S(1)}, u32[]{:S(2)}, u32[]{:S(2)}) collective-permute-start(bf16[1,352,128]{2,1,0:T(8,128)(2,1)S(1)} %get-tuple-element.33), channel_id=1, source_target_pairs={{1,0},{2,1},{3,2},{4,3},{5,4},{6,5},{7,6},{8,7},{9,8},{10,9},{11,1... | collective-permute-start | bytes 270344 | tf_op jit(solution)/shard_map/ppermute | solution.py:16
  153.1 8.5 %copy-start.12 = (bf16[16,352,128]{2,1,0:T(8,128)(2,1)S(1)}, bf16[16,352,128]{2,1,0:T(8,128)(2,1)}, u32[]{:S(2)}) copy-start(bf16[16,352,128]{2,1,0:T(8,128)(2,1)} %param.10) | copy-start | bytes 4325380
  161.6 5.8 %copy-start.1 = (bf16[16,352,512]{2,1,0:T(8,128)(2,1)S(1)}, bf16[16,352,512]{2,1,0:T(8,128)(2,1)}, u32[]{:S(2)}) copy-start(bf16[16,352,512]{2,1,0:T(8,128)(2,1)} %copy.23) | copy-start | bytes 17301508
  161.6 5.8 %copy-start.14 = (pred[16,352,128]{2,1,0:T(32,128)(4,1)S(1)}, pred[16,352,128]{2,1,0:T(32,128)(4,1)}, u32[]{:S(2)}) copy-start(pred[16,352,128]{2,1,0:T(32,128)(4,1)} %broadcast_compare_fusion) | copy-start | bytes 2162692
  161.6 5.8 %copy-start.16 = (bf16[128,512]{1,0:T(8,128)(2,1)S(1)}, bf16[128,512]{1,0:T(8,128)(2,1)}, u32[]{:S(2)}) copy-start(bf16[128,512]{1,0:T(8,128)(2,1)} %param.15) | copy-start | bytes 393220
  167.5 1.7 copy-start.10
  169.2 1.4 copy-start.9
  170.5 1.4 copy-start.8
  171.9 1.4 copy-start.7
  173.3 1.4 copy-start.4
  175.2 1.4 copy-start.6
  176.6 1.4 copy-start.5
  177.9 1.4 copy-start.3
  179.9 5.2 %collective-permute-start = (bf16[1,352,128]{2,1,0:T(8,128)(2,1)S(1)}, bf16[1,352,128]{2,1,0:T(8,128)(2,1)S(1)}, u32[]{:S(2)}, u32[]{:S(2)}) collective-permute-start(bf16[1,352,128]{2,1,0:T(8,128)(2,1)S(1)} %get-tuple-element.36), channel_id=1, source_target_pairs={{0,1},{1,2},{2,3},{3,4},{4,5},{5,6},{6,7},{7,8},{8,9},{9,10},{10,1... | collective-permute-start | bytes 270344 | tf_op jit(solution)/shard_map/ppermute | solution.py:15
  182.6 11.0 %collective-permute-start.1 = (bf16[1,352,128]{2,1,0:T(8,128)(2,1)S(1)}, bf16[1,352,128]{2,1,0:T(8,128)(2,1)S(1)}, u32[]{:S(2)}, u32[]{:S(2)}) collective-permute-start(bf16[1,352,128]{2,1,0:T(8,128)(2,1)S(1)} %get-tuple-element.37), channel_id=1, source_target_pairs={{1,0},{2,1},{3,2},{4,3},{5,4},{6,5},{7,6},{8,7},{9,8},{10,9},{11,1... | collective-permute-start | bytes 270344 | tf_op jit(solution)/shard_map/ppermute | solution.py:16
  184.8 183.4 %reduce-scatter.4.cloned.1.call-start = ((), (), s32[]{:S(2)}) async-start(), calls=%async_computation.2 | async-start | bytes 278528
  194.1 2.4 copy-start.15
  200.5 1.1 copy-start.13
  200.5 2.4 slice-start
  201.6 2.0 slice-start.1
Sparse Core Ops, SparseCore 0:
  184.9 124.6 all-reduce.4
  313.1 55.1 reduce-scatter.3
where the time goes:
time: 378 us; the launch traced here: 377 us
  waiting for transfers between devices  254 us (67%)
  local copies, waits for them, and re-layouts  48.8 us (13%)
  matrix products  25.6 us (7%)
  other arithmetic  18 us (5%)
  starting transfers between devices  15.5 us (4%)
  between operations  14.4 us (4%)
    psum x1, waiting for transfers between devices, shards(): middle_total = lax.psum(middle_part, 'rows')  97.3 us
    all_to_all x1, waiting for transfers between devices, shards(): lax.all_to_all(output_grad, 'rows', split_axis=0, concat_axis=2, tiled=True)  93.3 us
    unnamed x3, waiting for transfers between devices  55.1 us
    unnamed x43, local copies, waits for them, and re-layouts  27.6 us
    dot_general x11, matrix products, contract_rows(): lax.dot_general(left, right, (((0,), (0,)), ((), ())), preferred_element_...  12 us
    ppermute x2, waiting for transfers between devices, with_halo(): after = lax.ppermute(leading, axis, down)  8.54 us
    select_n x1, local copies, waits for them, and re-layouts, shards(): masked_out = jnp.where(output_pre > 0, spatial, jnp.zeros_like(spatial))  8.53 us
    select_n x1, other arithmetic, shards(): masked_out = jnp.where(output_pre > 0, spatial, jnp.zeros_like(spatial))  8.04 us
  transfers between devices with their start and end apart: 7, of which 4 were waited for; matrix products, arithmetic and copies ran while one was open for 10% of the time, Pallas kernels for 0%

commit v1 on v0

--- a/solution.py
+++ b/solution.py
@@ -3,6 +3,12 @@
 import jax.numpy as jnp
 from jax import lax
 from jax.sharding import PartitionSpec as P
+
+
+def add_all(x, name):
+    terms = lax.all_gather(x, name, axis=0, tiled=False)
+    total = terms.sum(axis=0)
+    return total
 
 
 def with_halo(value, sides, width):
@@ -97,7 +103,7 @@
         .astype(jnp.bfloat16)
         .reshape(tile_rows, map_cols, channels)
     )
-    middle_total = lax.psum(middle_part, "rows")
+    middle_total = add_all(middle_part, "rows")
     return (input_grad, first_wgrad, middle_total * factor, last_total * factor)
 
 

time: 378 us -> 442 us (1.17)
  waiting for transfers between devices: 254 us -> 311 us
  matrix products: 25.6 us -> 32.3 us
    all_gather x0 -> x1, waiting for transfers between devices: none -> 81.8 us  [add_all(): terms = lax.all_gather(x, name, axis=0, tiled=False)]
    psum x1, waiting for transfers between devices: 97.3 us -> 75.5 us  [shards(): last_total = lax.psum(last_part, 'rows')]
    ppermute x2, waiting for transfers between devices: 8.54 us -> 2.88 us  [with_halo(): after = lax.ppermute(leading, axis, down)]
    unnamed x43 -> x45, local copies, waits for them, and re-layouts: 27.6 us -> 24.8 us
    unnamed x3 -> x4, waiting for transfers between devices: 55.1 us -> 57.7 us
  transfers between devices with their start and end apart: 7 -> 8, of which waited for: 4 -> 5; matrix products, arithmetic and copies ran while one was open for 10% -> 12% of each run, Pallas kernels for 0% -> 0%
where the time goes in v1:
time: 442 us; the launch traced here: 441 us
  waiting for transfers between devices  311 us (70%)
  local copies, waits for them, and re-layouts  46.2 us (10%)
  matrix products  32.3 us (7%)
  other arithmetic  21.6 us (5%)
  starting transfers between devices  15.8 us (4%)
  between operations  14.1 us (3%)
    all_to_all x1, waiting for transfers between devices, shards(): lax.all_to_all(output_grad, 'rows', split_axis=0, concat_axis=2, tiled=True)  93 us
    all_gather x1, waiting for transfers between devices, add_all(): terms = lax.all_gather(x, name, axis=0, tiled=False)  81.8 us
    psum x1, waiting for transfers between devices, shards(): last_total = lax.psum(last_part, 'rows')  75.5 us
    unnamed x4, waiting for transfers between devices  57.7 us
    unnamed x45, local copies, waits for them, and re-layouts  24.8 us
    dot_general x11, matrix products, contract_rows(): lax.dot_general(left, right, (((0,), (0,)), ((), ())), preferred_element_...  15.8 us
  transfers between devices with their start and end apart: 8, of which 5 were waited for; matrix products, arithmetic and copies ran while one was open for 12% of the time, Pallas kernels for 0%

profile of v1, /device:TPU:0, one launch (start us, length us, event | category | flops | bytes accessed | tf_op | source)
XLA Modules:
  0.0 441.0 jit_solution(7111158011106145655)
XLA Ops:
  7.2 9.7 %copy.21 = bf16[256,352,32]{1,2,0:T(8,128)(2,1)} copy(bf16[256,352,32]{0,2,1:T(8,128)(2,1)} %param.12) | data formatting | bytes 11534336 | tf_op args[4]
  16.9 7.6 %all-to-all-start = ((bf16[256,352,32]{1,2,0:T(8,128)(2,1)}), bf16[256,352,32]{1,2,0:T(8,128)(2,1)}, u32[]{:S(2)}, u32[]{:S(2)}) async-start(bf16[256,352,32]{1,2,0:T(8,128)(2,1)} %copy.21), calls=%async_computation | async-start | bytes 12582912 | tf_op jit(solution)/shard_map/all_to_all | solution.py:47
  24.6 2.4 collective-permute-start.2
  27.1 1.3 collective-permute-start.3
  28.4 1.3 broadcast_compare_fusion.1
  29.6 1.3 broadcast_compare_fusion
  30.9 8.3 %copy.20 = bf16[16,352,512]{1,2,0:T(8,128)(2,1)} copy(bf16[16,352,512]{2,1,0:T(8,128)(2,1)} %param.11) | data formatting | bytes 11534336 | tf_op args[3]
  39.2 1.9 pad_maximum_fusion.1
  41.6 4.0 fusion.33
  45.6 93.0 %all-to-all-done = bf16[256,352,32]{1,2,0:T(8,128)(2,1)} async-done(((bf16[256,352,32]{1,2,0:T(8,128)(2,1)}), bf16[256,352,32]{1,2,0:T(8,128)(2,1)}, u32[]{:S(2)}, u32[]{:S(2)}) %all-to-all-start) | async-done | bytes 5767200 | tf_op jit(solution)/shard_map/all_to_all | solution.py:47
  138.7 6.4 %copy.22 = bf16[16,352,16,32]{1,3,2,0:T(8,128)(2,1)} copy(bf16[16,352,16,32]{1,3,0,2:T(8,128)(2,1)} %bitcast.3) | data formatting | bytes 11534336 | tf_op jit(solution)/shard_map/all_to_all | solution.py:47
  145.1 8.1 %compare_select_fusion = bf16[16,352,512]{1,2,0:T(8,128)(2,1)} fusion(bf16[16,352,512]{1,2,0:T(8,128)(2,1)} %copy.20, bf16[16,352,16,32]{1,3,2,0:T(8,128)(2,1)} %copy.22), kind=kLoop, calls=%fused_computation | loop fusion | flops 5767168 | bytes 17301504 | tf_op jit(solution)/shard_map/jit(_where)/select_n | solution.py:48
  153.2 5.7 %fusion.8 = f32[128,512]{1,0:T(8,128)} fusion(bf16[16,352,512]{1,2,0:T(8,128)(2,1)} %compare_select_fusion, bf16[16,352,128]{2,1,0:T(8,128)(2,1)S(1)} %copy-done.10), kind=kOutput, calls=%fused_computation.28 | convolution fusion | flops 738918400 | bytes 7471104 | tf_op jit(solution)/shard_map/dot_general | solution.py:28
  158.9 8.5 %copy.23 = bf16[16,352,512]{2,1,0:T(8,128)(2,1)} copy(bf16[16,352,512]{1,2,0:T(8,128)(2,1)} %compare_select_fusion) | data formatting | bytes 11534336 | tf_op jit(solution)/shard_map/jit(_where)/select_n | solution.py:48
  167.5 4.6 %fusion.3 = bf16[5632,128]{1,0:T(8,128)(2,1)S(1)} fusion(pred[5632,128]{1,0:T(32,128)(4,1)} %bitcast.150, bf16[5632,512]{1,0:T(8,128)(2,1)} %bitcast.125, bf16[128,512]{1,0:T(8,128)(2,1)S(1)} %copy-done.17), kind=kOutput, calls=%fused_computation.13 | convolution fusion | flops 739639296 | bytes 8060928 | tf_op jit(solution)/shard_map/dot_general | solution.py:54
  172.1 1.2 convolution_bitcast_fusion.2
  173.3 0.6 convolution_bitcast_fusion.5
  173.9 0.8 copy-done.2
  174.7 0.6 convolution_bitcast_fusion.8
  175.2 2.7 collective-permute-start
  177.9 1.5 collective-permute-start.1
  179.4 0.6 convolution_bitcast_fusion.9
  180.0 0.8 copy-done.7
  180.8 1.2 convolution_bitcast_fusion.3
  182.2 0.6 convolution_bitcast_fusion.4
  182.7 0.8 copy-done.5
  183.5 1.2 convolution_bitcast_fusion.6
  184.9 1.2 convolution_bitcast_fusion.7
  186.1 2.9 collective-permute-done.1
  189.4 2.4 fusion.34
  193.1 0.6 convolution_add_fusion.5
  195.3 0.6 convolution_add_fusion.2
  195.9 0.6 convolution_add_fusion.1
  197.0 0.8 fusion.2
  198.3 0.7 slice-done.1
  199.0 1.0 convolution_bitcast_fusion
  200.0 0.8 copy.27
  201.2 2.0 convolution_bitcast_fusion.1
  203.3 0.9 pad_maximum_fusion.4
  204.1 6.8 %add_convert_fusion = bf16[5632,512]{1,0:T(8,128)(2,1)} fusion(bf16[5632,512]{1,0:T(8,128)(2,1)} %bitcast.126, bf16[5632,128]{1,0:T(8,128)(2,1)S(1)} %fusion.2, bf16[512,128]{1,0:T(8,128)(2,1)S(1)} %copy-done), kind=kOutput, calls=%fused_computation.1 | convolution fusion | flops 746848256 | bytes 13107200 | tf_op jit(solution)/shard_map/dot_general | solution.py:98
  211.0 75.5 %all-reduce.4.cloned.1.call-done = f32[128,512]{1,0:T(8,128)} async-done(((f32[128,512]{1,0:T(8,128)}), f32[128,512]{1,0:T(8,128)}) %all-reduce.4.cloned.1.call-update) | async-done | bytes 262160 | tf_op jit(solution)/shard_map/psum | solution.py:53
  286.5 1.7 broadcast_multiply_fusion.1
  288.2 57.7 %reduce-scatter.4.cloned.1.call-done = f32[32,128]{1,0:T(8,128)} async-done(((f32[512,128]{1,0:T(8,128)}), f32[32,128]{1,0:T(8,128)}) %reduce-scatter.4.cloned.1.call-update) | async-done | bytes 16400
  345.9 0.8 copy.28
  346.7 0.7 copy.25
  347.4 81.8 %all-gather.3.cloned.1.call-done = f32[48,3,128,128]{3,2,1,0:T(8,128)} async-done(((f32[3,3,128,128]{3,2,1,0:T(8,128)}), f32[48,3,128,128]{3,2,1,0:T(8,128)}) %all-gather.3.cloned.1.call-update) | async-done | bytes 9437200 | tf_op jit(solution)/shard_map/all_gather | solution.py:9
  429.2 4.4 reduce_sum.9
  433.6 0.9 broadcast_multiply_fusion
  (60 shorter events, 5.8 us)
Async XLA Ops:
  7.2 197.0 %copy-start = (bf16[512,128]{1,0:T(8,128)(2,1)S(1)}, bf16[512,128]{1,0:T(8,128)(2,1)}, u32[]{:S(2)}) copy-start(bf16[512,128]{1,0:T(8,128)(2,1)} %param.13) | copy-start | bytes 393220
  16.9 7.6 %copy-start.1 = (bf16[16,352,128]{2,1,0:T(8,128)(2,1)S(1)}, bf16[16,352,128]{2,1,0:T(8,128)(2,1)}, u32[]{:S(2)}) copy-start(bf16[16,352,128]{2,1,0:T(8,128)(2,1)} %param.9) | copy-start | bytes 4325380
  16.9 121.8 %all-to-all-start = ((bf16[256,352,32]{1,2,0:T(8,128)(2,1)}), bf16[256,352,32]{1,2,0:T(8,128)(2,1)}, u32[]{:S(2)}, u32[]{:S(2)}) async-start(bf16[256,352,32]{1,2,0:T(8,128)(2,1)} %copy.21), calls=%async_computation | async-start | bytes 12582912 | tf_op jit(solution)/shard_map/all_to_all | solution.py:47
  24.5 262.0 %all-reduce.4.cloned.1.call-start = ((), (), s32[]{:S(2)}) async-start(), calls=%async_computation.2 | async-start | bytes 524288 | tf_op jit(solution)/shard_map/psum | solution.py:53
  24.6 5.0 %copy-start.9 = (bf16[16,352,128]{2,1,0:T(8,128)(2,1)S(1)}, bf16[16,352,128]{2,1,0:T(8,128)(2,1)}, u32[]{:S(2)}) copy-start(bf16[16,352,128]{2,1,0:T(8,128)(2,1)} %param.10) | copy-start | bytes 4325380
  24.6 14.6 %collective-permute-start.2 = (bf16[1,352,128]{2,1,0:T(8,128)(2,1)S(1)}, bf16[1,352,128]{2,1,0:T(8,128)(2,1)S(1)}, u32[]{:S(2)}, u32[]{:S(2)}) collective-permute-start(bf16[1,352,128]{2,1,0:T(8,128)(2,1)S(1)} %get-tuple-element.30), channel_id=1, source_target_pairs={{0,1},{1,2},{2,3},{3,4},{4,5},{5,6},{6,7},{7,8},{8,9},{9,10},{10,1... | collective-permute-start | bytes 270344 | tf_op jit(solution)/shard_map/ppermute | solution.py:21
  27.1 12.2 %collective-permute-start.3 = (bf16[1,352,128]{2,1,0:T(8,128)(2,1)S(1)}, bf16[1,352,128]{2,1,0:T(8,128)(2,1)S(1)}, u32[]{:S(2)}, u32[]{:S(2)}) collective-permute-start(bf16[1,352,128]{2,1,0:T(8,128)(2,1)S(1)} %get-tuple-element.31), channel_id=1, source_target_pairs={{1,0},{2,1},{3,2},{4,3},{5,4},{6,5},{7,6},{8,7},{9,8},{10,9},{11,1... | collective-permute-start | bytes 270344 | tf_op jit(solution)/shard_map/ppermute | solution.py:22
  145.1 8.2 %copy-start.10 = (bf16[16,352,128]{2,1,0:T(8,128)(2,1)S(1)}, bf16[16,352,128]{2,1,0:T(8,128)(2,1)}, u32[]{:S(2)}) copy-start(bf16[16,352,128]{2,1,0:T(8,128)(2,1)} %param.10) | copy-start | bytes 4325380
  158.9 8.5 %copy-start.17 = (bf16[128,512]{1,0:T(8,128)(2,1)S(1)}, bf16[128,512]{1,0:T(8,128)(2,1)}, u32[]{:S(2)}) copy-start(bf16[128,512]{1,0:T(8,128)(2,1)} %param.15) | copy-start | bytes 393220
  167.4 178.5 %reduce-scatter.4.cloned.1.call-start = ((), (), s32[]{:S(2)}) async-start(), calls=%async_computation.4 | async-start | bytes 278528
  167.4 4.6 %copy-start.3 = (bf16[16,352,128]{2,1,0:T(8,128)(2,1)S(1)}, bf16[16,352,128]{2,1,0:T(8,128)(2,1)}, u32[]{:S(2)}) copy-start(bf16[16,352,128]{2,1,0:T(8,128)(2,1)} %get-tuple-element.29) | copy-start | bytes 4325380
  173.3 1.4 copy-start.2
  174.7 4.8 %copy-start.8 = (bf16[16,352,128]{2,1,0:T(8,128)(2,1)S(1)}, bf16[16,352,128]{2,1,0:T(8,128)(2,1)}, u32[]{:S(2)}) copy-start(bf16[16,352,128]{2,1,0:T(8,128)(2,1)} %get-tuple-element.16) | copy-start | bytes 4325380
  175.2 10.8 %collective-permute-start = (bf16[1,352,128]{2,1,0:T(8,128)(2,1)S(1)}, bf16[1,352,128]{2,1,0:T(8,128)(2,1)S(1)}, u32[]{:S(2)}, u32[]{:S(2)}) collective-permute-start(bf16[1,352,128]{2,1,0:T(8,128)(2,1)S(1)} %get-tuple-element.34), channel_id=1, source_target_pairs={{0,1},{1,2},{2,3},{3,4},{4,5},{5,6},{6,7},{7,8},{8,9},{9,10},{10,1... | collective-permute-start | bytes 270344 | tf_op jit(solution)/shard_map/ppermute | solution.py:21
  177.9 11.0 %collective-permute-start.1 = (bf16[1,352,128]{2,1,0:T(8,128)(2,1)S(1)}, bf16[1,352,128]{2,1,0:T(8,128)(2,1)S(1)}, u32[]{:S(2)}, u32[]{:S(2)}) collective-permute-start(bf16[1,352,128]{2,1,0:T(8,128)(2,1)S(1)} %get-tuple-element.35), channel_id=1, source_target_pairs={{1,0},{2,1},{3,2},{4,3},{5,4},{6,5},{7,6},{8,7},{9,8},{10,9},{11,1... | collective-permute-start | bytes 270344 | tf_op jit(solution)/shard_map/ppermute | solution.py:22
  179.4 1.4 copy-start.7
  180.8 1.4 copy-start.6
  182.2 1.4 copy-start.5
  183.5 1.4 copy-start.4
  189.4 2.4 copy-start.12
  195.8 1.1 copy-start.11
  195.9 2.4 slice-start
  197.0 2.0 slice-start.1
  200.8 228.4 %all-gather.3.cloned.1.call-start = ((), (), s32[]{:S(2)}) async-start(), calls=%async_computation.3 | async-start | bytes 10027008 | tf_op jit(solution)/shard_map/all_gather | solution.py:9
  201.1 2.0 copy-start.15
  201.1 2.0 copy-start.16
  201.1 2.1 copy-start.13
  201.1 2.1 copy-start.14
Sparse Core Ops, SparseCore 0:
  167.5 118.9 all-reduce.3
  290.0 55.8 reduce-scatter.3
  348.7 80.4 all-gather.2
